TPU v7x, 512 devices: a whole 4x4x16 slice. The times are simulated.
512 devices in a mesh: img: 16 (over y, z_hi, core), ref: 32 (over z_lo, x).
Axes of the slice: x: 4, y: 4, z: 16 (z_hi: 2, z_lo: 8; z = z_hi * 8 + z_lo), core: 2. Of those that a mesh axis runs over, the one named last changes fastest.
Arguments:
- images: float32 [2, 256, 32768], P(None, 'img', 'ref'), may hold values from -6 to 6
- references: float32 [2, 256, 32768], P(None, 'ref', 'img'), may hold values from -2 to 2
- precision: float32 [256], P('img'), may hold values from 0.00390625 to 0.0390625
- shifts: int32 [12, 2], replicated, may hold values from -6 to 6, as said below
- labels: int32 [256], P('ref'), may hold values from 0 to 3
- log_prior: float32 [4], replicated, may hold values from -4 to 4
Outputs:
- new_refs: float32 [2, 256, 32768], P(None, 'ref', 'img')
- class_post: float32 [256, 4], P('img')
Inputs may be any that keep to these rules, and one draw needn't show every extreme that they name: `shifts`: both ends of the range occur in every draw.
All inputs are finite; a program needn't handle non-finite values.
Results may differ from a plain program's by a relative error of at most 0.0056.
Values may be sent and summed in bfloat16 or wider, within the bound.
No kernel may reach another device: no remote copies, remote signals or barrier semaphores. Data moves between devices by JAX's collectives and lax.ppermute only.
A program may use at most 64 MiB of HBM per device.

v0:
```python
import math
import jax
import jax.numpy as jnp
from jax import lax
from jax.sharding import PartitionSpec as P

ROWS = 256
COLS = 128
SHIFTS = 12
CLASSES = 4


def phases(shifts):
    index = jnp.arange(ROWS * COLS, dtype=jnp.int32)
    freq_y = (index // COLS - ROWS // 2).astype(jnp.float32)
    freq_x = (index % COLS).astype(jnp.float32)
    shift_x = shifts[:, 0].astype(jnp.float32)[:, None]
    shift_y = shifts[:, 1].astype(jnp.float32)[:, None]
    angles = 2.0 * math.pi / ROWS * (freq_x[None, :] * shift_x + freq_y[None, :] * shift_y)
    return (jnp.cos(angles), jnp.sin(angles))


def inner_rows(left, right):
    return lax.dot_general(
        left, right, (((1,), (1,)), ((), ())), preferred_element_type=jnp.float32
    )


def inner_cols(left, right):
    return lax.dot_general(
        left, right, (((0,), (0,)), ((), ())), preferred_element_type=jnp.float32
    )


def local(images, references, precision, shifts, labels, log_prior):
    img_low = lax.all_gather(images.astype(jnp.bfloat16), "ref", axis=2, tiled=True)
    ref_low = lax.all_gather(references.astype(jnp.bfloat16), "img", axis=2, tiled=True)
    pixels = img_low.shape[2]
    img_dev = img_low.shape[1]
    ref_dev = ref_low.shape[1]
    blocks = SHIFTS // 4
    cosine, sine_part = phases(shifts)
    cos_blocks = cosine.reshape(blocks, 4, pixels)
    sin_blocks = sine_part.reshape(blocks, 4, pixels)
    ref_wide = ref_low.astype(jnp.float32)
    energy = jnp.sum(ref_wide * ref_wide, axis=(0, 2))
    onehot = (labels[:, None] == jnp.arange(CLASSES, dtype=jnp.int32)[None, :]).astype(jnp.float32)
    prior_term = jnp.sum(onehot * log_prior[None, :], axis=1)

    def cross_block(operands):
        cos_rows, sin_rows = operands
        shifted_re = (
            ref_wide[0][None] * cos_rows[:, None, :] + ref_wide[1][None] * sin_rows[:, None, :]
        ).astype(jnp.bfloat16)
        shifted_im = (
            ref_wide[1][None] * cos_rows[:, None, :] - ref_wide[0][None] * sin_rows[:, None, :]
        ).astype(jnp.bfloat16)
        return inner_rows(img_low[0], shifted_re.reshape(4 * ref_dev, pixels)) + inner_rows(
            img_low[1], shifted_im.reshape(4 * ref_dev, pixels)
        )

    cross_terms = lax.map(cross_block, (cos_blocks, sin_blocks))
    cross_terms = jnp.transpose(cross_terms, (1, 0, 2)).reshape(img_dev, SHIFTS, ref_dev)
    scores = (
        precision[:, None, None] * (cross_terms - 0.5 * energy[None, None, :])
        + prior_term[None, None, :]
    )
    local_top = jnp.max(scores, axis=(1, 2))
    top_score = lax.pmax(local_top, "ref")
    exponent = jnp.exp(scores - top_score[:, None, None])
    local_class = jnp.einsum(
        "ik,kc->ic", jnp.sum(exponent, axis=1), onehot, precision=lax.Precision.HIGHEST
    )
    row_total, class_sum = lax.psum((jnp.sum(exponent, axis=(1, 2)), local_class), "ref")
    posterior = exponent / row_total[:, None, None]
    class_post = class_sum / row_total[:, None]
    local_mass = jnp.sum(posterior, axis=(0, 1))
    post_low = posterior.astype(jnp.bfloat16).reshape(img_dev, blocks, 4 * ref_dev)
    post_low = jnp.transpose(post_low, (1, 0, 2))

    def back_block(running, operands):
        weights_blk, cos_rows, sin_rows = operands
        back_re = inner_cols(weights_blk, img_low[0]).reshape(4, ref_dev, pixels)
        back_im = inner_cols(weights_blk, img_low[1]).reshape(4, ref_dev, pixels)
        part_re = jnp.sum(back_re * cos_rows[:, None, :] - back_im * sin_rows[:, None, :], axis=0)
        part_im = jnp.sum(back_im * cos_rows[:, None, :] + back_re * sin_rows[:, None, :], axis=0)
        return (running + jnp.stack([part_re, part_im]), None)

    start_sum = jnp.zeros((2, ref_dev, pixels), jnp.float32)
    summed, unused = lax.scan(back_block, start_sum, (post_low, cos_blocks, sin_blocks))
    summed_all, ref_mass = lax.psum((summed, local_mass), "img")
    pix_block = pixels // lax.axis_size("img")
    summed_part = lax.dynamic_slice_in_dim(
        summed_all, lax.axis_index("img") * pix_block, pix_block, 2
    )
    new_refs = summed_part / (ref_mass + 1.0)[None, :, None]
    return (new_refs, class_post)


def solution(mesh):
    return jax.shard_map(
        local,
        mesh=mesh,
        in_specs=(P(None, "img", "ref"), P(None, "ref", "img"), P("img"), P(), P("ref"), P()),
        out_specs=(P(None, "ref", "img"), P("img", None)),
        check_vma=False,
    )
```

profile of v0, /device:TPU:102, one launch (start us, length us, event | category | flops | bytes accessed | tf_op | source)
XLA Modules:
  0.0 916.9 jit_solution(10611607265250826830)
XLA Ops:
  7.2 1.5 convert_element_type.63
  8.8 1.5 convert_element_type.69
  12.3 12.6 %fusion.39 = (f32[3,4,32768]{2,1,0:T(4,128)}, f32[3,4,32768]{2,1,0:T(4,128)}) fusion(f32[3,4]{1,0:T(4,128)S(1)} %mul.207, f32[32768]{0:T(1024)S(1)} %get-tuple-element.128, f32[3,4]{1,0:T(4,128)S(1)} %mul.203, f32[32768]{0:T(1024)S(1)} %get-tuple-element.127), kind=kLoop, calls=%fused_computation.44 | loop fusion | flops 1572864 | bytes 3407968 | tf_op jit(solution)/shard_map/sin | solution.py:20
  24.9 59.6 %all-gather.3.cloned.1.call-done = bf16[2,8,32768]{2,1,0:T(8,128)(2,1)} async-done(((bf16[2,8,2048]{2,1,0:T(8,128)(2,1)}), bf16[2,8,32768]{2,1,0:T(8,128)(2,1)}) %all-gather.3.cloned.1.call-update) | async-done | bytes 1048592 | tf_op jit(solution)/shard_map/all_gather | solution.py:37
  84.5 1.9 multiply_reduce_fusion
  86.5 2.7 convert_element_type.64
  89.2 173.8 %all-gather.5.cloned.1.call-done = bf16[2,16,32768]{2,1,0:T(8,128)(2,1)} async-done(((bf16[2,16,1024]{2,1,0:T(8,128)(2,1)}), bf16[2,16,32768]{2,1,0:T(8,128)(2,1)}) %all-gather.5.cloned.1.call-update) | async-done | bytes 2097168 | tf_op jit(solution)/shard_map/all_gather | solution.py:36
  263.0 14.6 %while.21 = (s32[]{:T(128)}, f32[3,16,32]{2,1,0:T(8,128)S(1)}, f32[2,8,32768]{2,1,0:T(8,128)}, f32[3,4,32768]{2,1,0:T(4,128)}, f32[3,4,32768]{2,1,0:T(4,128)}, /*index=5*/bf16[2,16,32768]{2,1,0:T(8,128)(2,1)}, s32[]{:T(128)}) while((s32[]{:T(128)}, f32[3,16,32]{2,1,0:T(8,128)S(1)}, f32[2,8,32768]{2,1,0:T(8,128)}, f32[3,4,32768]{2,1,0:T(4,128)}, ...), condition=%wide.region_1.2_spmd, body=%wide.region_0.1_spmd.sunk | while | flops 75497984 | bytes 31475852 | solution.py:62
  265.0 1.4 copy-done.2
  277.8 100.4 %pmax.7 = f32[16]{0:T(128)S(1)} all-reduce(f32[16]{0:T(128)S(1)} %fusion.52), channel_id=1, replica_groups=mesh['img'=16,'ref'=32] {'ref'}, use_global_device_ids=true, to_apply=%region_5.6 | all-reduce | flops 16 | bytes 128 | tf_op jit(solution)/shard_map/pmax | solution.py:69
  378.5 122.7 %all-reduce = (f32[16]{0:T(128)S(1)}, f32[16,4]{0,1:T(4,128)S(1)}) all-reduce(f32[16]{0:T(128)S(1)} %fusion.51, f32[16,4]{0,1:T(4,128)S(1)} %fusion.53), channel_id=1, replica_groups=mesh['img'=16,'ref'=32] {'ref'}, use_global_device_ids=true, to_apply=%region_7.8 | all-reduce | flops 80 | bytes 640 | tf_op jit(solution)/shard_map/psum | solution.py:74
  501.3 25.5 %while.22 = (s32[]{:T(128)}, f32[2,8,32768]{2,1,0:T(8,128)S(1)}, bf16[3,16,32]{1,2,0:T(8,128)(2,1)S(1)}, bf16[2,16,32768]{2,1,0:T(8,128)(2,1)}, f32[3,4,32768]{2...) while((s32[]{:T(128)}, f32[2,8,32768]{2,1,0:T(8,128)S(1)}, ...), condition=%wide.region_11.12_spmd.clone, body=%wide.region_8.11_spmd.clone.sunk | while | flops 76546048 | bytes 30425728 | solution.py:90
  501.3 1.9 fusion.73
  505.1 2.8 subtract_reduce_fusion.2
  507.9 1.8 maximum_add_fusion.2
  509.8 1.9 fusion.73
  513.6 2.8 subtract_reduce_fusion.2
  516.4 1.8 maximum_add_fusion.2
  518.2 1.9 fusion.73
  522.1 2.8 subtract_reduce_fusion.2
  524.9 1.8 maximum_add_fusion.2
  528.3 62.1 %psum.30 = f32[8]{0:T(128)S(1)} all-reduce(f32[8]{0:T(128)S(1)} %reduce_sum.75), channel_id=1, replica_groups=mesh['img'=16,'ref'=32] {'img'}, use_global_device_ids=true, to_apply=%region_15.16 | all-reduce | flops 8 | bytes 64 | tf_op jit(solution)/shard_map/psum | solution.py:91
  591.0 317.7 %all-reduce.3.cloned.1.call-done = f32[2,8,32768]{2,1,0:T(8,128)} async-done(((f32[2,8,32768]{2,1,0:T(8,128)}), f32[2,8,32768]{2,1,0:T(8,128)}) %all-reduce.3.cloned.1.call-update) | async-done | bytes 2097168 | tf_op jit(solution)/shard_map/psum | solution.py:91
  908.7 1.6 dynamic-slice_divide_fusion
  (67 shorter events, 23.6 us)
Async XLA Ops:
  7.2 77.4 %all-gather.3.cloned.1.call-start = ((), (), s32[]{:S(2)}) async-start(), calls=%async_computation | async-start | bytes 1114112 | tf_op jit(solution)/shard_map/all_gather | solution.py:37
  8.8 254.2 %all-gather.5.cloned.1.call-start = ((), (), s32[]{:S(2)}) async-start(), calls=%async_computation.1 | async-start | bytes 2162688 | tf_op jit(solution)/shard_map/all_gather | solution.py:36
  10.4 898.3 %all-reduce.3.cloned.1.call-start = ((), (), s32[]{:S(2)}) async-start(), calls=%async_computation.2 | async-start | bytes 4194304 | tf_op jit(solution)/shard_map/psum | solution.py:91
  262.9 14.7 %copy-start.4 = (f32[16]{0:T(128)S(1)}, f32[16]{0:T(128)}, u32[]{:S(2)}) copy-start(f32[16]{0:T(128)} %param.12) | copy-start | bytes 196
  262.9 115.4 %copy-start.5 = (s32[8]{0:T(128)S(1)}, s32[8]{0:T(128)}, u32[]{:S(2)}) copy-start(s32[8]{0:T(128)} %param.14) | copy-start | bytes 100
  263.0 1.9 copy-start.1
  264.9 1.6 copy-start.2
  267.9 1.9 copy-start.1
  269.8 1.6 copy-start.2
  272.7 1.9 copy-start.1
  274.6 1.6 copy-start.2
  503.2 1.9 copy-start.3
  511.7 1.9 copy-start.3
  520.2 1.9 copy-start.3
  526.7 1.3 copy-start
Sparse Core Ops, SparseCore 0:
  11.9 72.5 all-gather.2
  86.6 176.2 all-gather.4
  528.2 380.4 all-reduce.2
where the time goes:
time: 918 us; the launch traced here: 917 us
  waiting for transfers between devices  551 us (60%)
  blocking collectives  285 us (31%)
  other arithmetic  30.1 us (3%)
  matrix products  18.4 us (2%)
  local copies, waits for them, and re-layouts  18 us (2%)
  between operations  13.8 us (2%)
    psum x1, waiting for transfers between devices, local(): summed_all, ref_mass = lax.psum((summed, local_mass), 'img')  318 us
    all_gather x1, waiting for transfers between devices, local(): lax.all_gather(images.astype(jnp.bfloat16), 'ref', axis=2, tiled=True)  174 us
    psum x1, blocking collectives, local(): lax.psum((jnp.sum(exponent, axis=(1, 2)), local_class), 'ref')  123 us
    pmax x1, blocking collectives, local(): top_score = lax.pmax(local_top, 'ref')  100 us
    psum x1, blocking collectives, local(): summed_all, ref_mass = lax.psum((summed, local_mass), 'img')  62.1 us
    all_gather x1, waiting for transfers between devices, local(): lax.all_gather(references.astype(jnp.bfloat16), 'img', axis=2, tiled=True)  59.6 us
  transfers between devices with their start and end apart: 3, of which 3 were waited for; matrix products, arithmetic and copies ran while one was open for 2% of the time, Pallas kernels for 0%

commit v1 on v0

--- a/solution.py
+++ b/solution.py
@@ -33,7 +33,12 @@
 
 
 def local(images, references, precision, shifts, labels, log_prior):
-    img_low = lax.all_gather(images.astype(jnp.bfloat16), "ref", axis=2, tiled=True)
+    img_low = jnp.concatenate(
+        lax.all_to_all(
+            jnp.stack([images.astype(jnp.bfloat16)] * lax.axis_size("ref")), "ref", 0, 0
+        ),
+        axis=2,
+    )
     ref_low = lax.all_gather(references.astype(jnp.bfloat16), "img", axis=2, tiled=True)
     pixels = img_low.shape[2]
     img_dev = img_low.shape[1]

time: 918 us -> 746 us (0.81)
  waiting for transfers between devices: 551 us -> 408 us
  blocking collectives: 285 us -> 239 us
  starting transfers between devices: 0.12 us -> 14.5 us
    all_gather x1 -> x0, waiting for transfers between devices: 174 us -> none  [local(): lax.all_gather(images.astype(jnp.bfloat16), 'ref', axis=2, tiled=True)]
    pmax x1, blocking collectives: 100 us -> 71.2 us  [local(): top_score = lax.pmax(local_top, 'ref')]
    all_gather x1, waiting for transfers between devices: 59.6 us -> 77 us  [local(): lax.all_gather(references.astype(jnp.bfloat16), 'img', axis=2, tiled=True)]
    psum x1, blocking collectives: 123 us -> 106 us  [local(): lax.psum((jnp.sum(exponent, axis=(1, 2)), local_class), 'ref')]
    all_to_all x0 -> x1, starting transfers between devices: none -> 14.4 us  [local(): lax.all_to_all(jnp.stack([images.astype(jnp.bfloat16)] * lax.axis_size('r...]
  transfers between devices with their start and end apart: 3 -> 3, of which waited for: 3 -> 3; matrix products, arithmetic and copies ran while one was open for 2% -> 3% of each run, Pallas kernels for 0% -> 0%
where the time goes in v1:
time: 746 us; the launch traced here: 745 us
  waiting for transfers between devices  408 us (55%)
  blocking collectives  239 us (32%)
  other arithmetic  27.1 us (4%)
  local copies, waits for them, and re-layouts  22.7 us (3%)
  matrix products  18.4 us (2%)
  starting transfers between devices  14.5 us (2%)
  between operations  14.2 us (2%)
    psum x1, waiting for transfers between devices, local(): summed_all, ref_mass = lax.psum((summed, local_mass), 'img')  323 us
    psum x1, blocking collectives, local(): lax.psum((jnp.sum(exponent, axis=(1, 2)), local_class), 'ref')  106 us
    all_gather x1, waiting for transfers between devices, local(): lax.all_gather(references.astype(jnp.bfloat16), 'img', axis=2, tiled=True)  77 us
    pmax x1, blocking collectives, local(): top_score = lax.pmax(local_top, 'ref')  71.2 us
    psum x1, blocking collectives, local(): summed_all, ref_mass = lax.psum((summed, local_mass), 'img')  62 us
  transfers between devices with their start and end apart: 3, of which 3 were waited for; matrix products, arithmetic and copies ran while one was open for 3% of the time, Pallas kernels for 0%

profile of v1, /device:TPU:102, one launch (start us, length us, event | category | flops | bytes accessed | tf_op | source)
XLA Modules:
  0.0 744.8 jit_solution(9368254111765697503)
XLA Ops:
  8.1 1.6 stack.8
  9.7 14.4 %all-to-all-start = ((bf16[32,2,16,1024]{3,2,1,0:T(8,128)(2,1)}), bf16[32,2,16,1024]{3,2,1,0:T(8,128)(2,1)}, u32[]{:S(2)}, u32[]{:S(2)}) async-start(bf16[32,2,16,1024]{3,2,1,0:T(8,128)(2,1)} %stack.8), calls=%async_computation | async-start | bytes 4194304 | tf_op jit(solution)/shard_map/all_to_all | solution.py:37
  25.2 12.7 %fusion.39 = (f32[3,4,32768]{2,1,0:T(4,128)}, f32[3,4,32768]{2,1,0:T(4,128)}) fusion(f32[3,4]{1,0:T(4,128)S(1)} %mul.207, f32[32768]{0:T(1024)S(1)} %get-tuple-element.128, f32[3,4]{1,0:T(4,128)S(1)} %mul.203, f32[32768]{0:T(1024)S(1)} %get-tuple-element.127), kind=kLoop, calls=%fused_computation.44 | loop fusion | flops 1572864 | bytes 3407968 | tf_op jit(solution)/shard_map/sin | solution.py:20
  38.0 77.0 %all-gather.2.cloned.1.call-done = bf16[2,8,32768]{2,1,0:T(8,128)(2,1)} async-done(((bf16[2,8,2048]{2,1,0:T(8,128)(2,1)}), bf16[2,8,32768]{2,1,0:T(8,128)(2,1)}) %all-gather.2.cloned.1.call-update) | async-done | bytes 1048592 | tf_op jit(solution)/shard_map/all_gather | solution.py:42
  115.0 1.9 multiply_reduce_fusion
  117.0 2.7 convert_element_type.64
  119.7 8.6 %all-to-all-done = bf16[32,2,16,1024]{3,2,1,0:T(8,128)(2,1)} async-done(((bf16[32,2,16,1024]{3,2,1,0:T(8,128)(2,1)}), bf16[32,2,16,1024]{3,2,1,0:T(8,128)(2,1)}, u32[]{:S(2)}, u32[]{:S(2)}) %all-to-all-start) | async-done | bytes 2097184 | tf_op jit(solution)/shard_map/all_to_all | solution.py:37
  128.3 3.2 copy.19
  131.4 14.6 %while.21 = (s32[]{:T(128)}, f32[3,16,32]{2,1,0:T(8,128)S(1)}, f32[2,8,32768]{2,1,0:T(8,128)}, f32[3,4,32768]{2,1,0:T(4,128)}, f32[3,4,32768]{2,1,0:T(4,128)}, /*index=5*/bf16[2,16,32768]{2,1,0:T(8,128)(2,1)}, s32[]{:T(128)}) while((s32[]{:T(128)}, f32[3,16,32]{2,1,0:T(8,128)S(1)}, f32[2,8,32768]{2,1,0:T(8,128)}, f32[3,4,32768]{2,1,0:T(4,128)}, ...), condition=%wide.region_1.2_spmd, body=%wide.region_0.1_spmd.sunk | while | flops 75497984 | bytes 31475852 | solution.py:67
  146.3 71.2 %pmax.7 = f32[16]{0:T(128)S(1)} all-reduce(f32[16]{0:T(128)S(1)} %fusion.52), channel_id=1, replica_groups=mesh['img'=16,'ref'=32] {'ref'}, use_global_device_ids=true, to_apply=%region_5.6 | all-reduce | flops 16 | bytes 128 | tf_op jit(solution)/shard_map/pmax | solution.py:74
  217.8 106.1 %all-reduce = (f32[16]{0:T(128)S(1)}, f32[16,4]{0,1:T(4,128)S(1)}) all-reduce(f32[16]{0:T(128)S(1)} %fusion.51, f32[16,4]{0,1:T(4,128)S(1)} %fusion.53), channel_id=1, replica_groups=mesh['img'=16,'ref'=32] {'ref'}, use_global_device_ids=true, to_apply=%region_7.8 | all-reduce | flops 80 | bytes 640 | tf_op jit(solution)/shard_map/psum | solution.py:79
  323.9 25.5 %while.22 = (s32[]{:T(128)}, f32[2,8,32768]{2,1,0:T(8,128)S(1)}, bf16[3,16,32]{1,2,0:T(8,128)(2,1)S(1)}, bf16[2,16,32768]{2,1,0:T(8,128)(2,1)}, f32[3,4,32768]{2...) while((s32[]{:T(128)}, f32[2,8,32768]{2,1,0:T(8,128)S(1)}, ...), condition=%wide.region_11.12_spmd.clone, body=%wide.region_8.11_spmd.clone.sunk | while | flops 76546048 | bytes 30425728 | solution.py:95
  324.0 1.9 fusion.73
  327.8 2.8 subtract_reduce_fusion.2
  330.6 1.8 maximum_add_fusion.2
  332.4 1.9 fusion.73
  336.3 2.8 subtract_reduce_fusion.2
  339.1 1.8 maximum_add_fusion.2
  340.9 1.9 fusion.73
  344.7 2.8 subtract_reduce_fusion.2
  347.6 1.8 maximum_add_fusion.2
  351.0 62.0 %psum.30 = f32[8]{0:T(128)S(1)} all-reduce(f32[8]{0:T(128)S(1)} %reduce_sum.75), channel_id=1, replica_groups=mesh['img'=16,'ref'=32] {'img'}, use_global_device_ids=true, to_apply=%region_15.16 | all-reduce | flops 8 | bytes 64 | tf_op jit(solution)/shard_map/psum | solution.py:96
  413.6 322.8 %all-reduce.3.cloned.1.call-done = f32[2,8,32768]{2,1,0:T(8,128)} async-done(((f32[2,8,32768]{2,1,0:T(8,128)}), f32[2,8,32768]{2,1,0:T(8,128)}) %all-reduce.3.cloned.1.call-update) | async-done | bytes 2097168 | tf_op jit(solution)/shard_map/psum | solution.py:96
  736.4 1.6 dynamic-slice_divide_fusion
  (74 shorter events, 25.2 us)
Async XLA Ops:
  9.7 14.5 %copy-start.4 = (f32[2,8,2048]{2,1,0:T(8,128)S(1)}, f32[2,8,2048]{2,1,0:T(8,128)}, u32[]{:S(2)}) copy-start(f32[2,8,2048]{2,1,0:T(8,128)} %param.11) | copy-start | bytes 393220
  9.7 15.3 %copy-start.6 = (s32[12,2]{0,1:T(2,128)S(1)}, s32[12,2]{0,1:T(2,128)}, u32[]{:S(2)}) copy-start(s32[12,2]{0,1:T(2,128)} %param.13) | copy-start | bytes 292
  9.7 118.6 %all-to-all-start = ((bf16[32,2,16,1024]{3,2,1,0:T(8,128)(2,1)}), bf16[32,2,16,1024]{3,2,1,0:T(8,128)(2,1)}, u32[]{:S(2)}, u32[]{:S(2)}) async-start(bf16[32,2,16,1024]{3,2,1,0:T(8,128)(2,1)} %stack.8), calls=%async_computation | async-start | bytes 4194304 | tf_op jit(solution)/shard_map/all_to_all | solution.py:37
  24.2 13.7 %copy-start.7 = (s32[8]{0:T(128)S(1)}, s32[8]{0:T(128)}, u32[]{:S(2)}) copy-start(s32[8]{0:T(128)} %param.14) | copy-start | bytes 100
  24.2 13.7 %copy-start.8 = (f32[4]{0:T(128)S(1)}, f32[4]{0:T(128)}, u32[]{:S(2)}) copy-start(f32[4]{0:T(128)} %param.15) | copy-start | bytes 52
  24.2 90.8 %all-gather.2.cloned.1.call-start = ((), (), s32[]{:S(2)}) async-start(), calls=%async_computation.1 | async-start | bytes 1114112 | tf_op jit(solution)/shard_map/all_gather | solution.py:42
  24.9 711.5 %all-reduce.3.cloned.1.call-start = ((), (), s32[]{:S(2)}) async-start(), calls=%async_computation.2 | async-start | bytes 4194304 | tf_op jit(solution)/shard_map/psum | solution.py:96
  131.4 14.7 %copy-start.5 = (f32[16]{0:T(128)S(1)}, f32[16]{0:T(128)}, u32[]{:S(2)}) copy-start(f32[16]{0:T(128)} %param.12) | copy-start | bytes 196
  131.4 1.9 copy-start.1
  133.4 1.6 copy-start.2
  136.3 1.9 copy-start.1
  138.2 1.6 copy-start.2
  141.2 1.9 copy-start.1
  143.1 1.6 copy-start.2
  325.9 1.9 copy-start.3
  334.4 1.9 copy-start.3
  342.8 1.9 copy-start.3
  349.4 1.3 copy-start
Sparse Core Ops, SparseCore 0:
  28.9 86.0 all-gather.1
  350.8 385.4 all-reduce.2
